TPU v7x, 32 devices: a whole 2x2x4 slice. The times are simulated.
32 devices in a mesh: fsdp: 8 (over y, x, core), tp: 4 (over z).
Axes of the slice: x: 2, y: 2, z: 4, core: 2. Of those that a mesh axis runs over, the one named last changes fastest.
Arguments:
- features: bfloat16 [1024, 8192], P('fsdp'), may hold values from -17 to 17
- key_partials: bfloat16 [1024, 4, 128], P('fsdp', 'tp'), may hold values from -0.30935922 to 0.30935922
- momentum: float32 [4096, 4, 128], P('fsdp', 'tp'), may hold values from -6 to 6
Outputs:
- update: float32 [4096, 4, 128], P('fsdp', 'tp')
- new_momentum: float32 [4096, 4, 128], P('fsdp', 'tp')
All inputs are finite; a program needn't handle non-finite values.
Results may differ from a plain program's by a relative error of at most 0.0003.
Values may be sent and summed in bfloat16 or wider, within the bound.
No kernel may reach another device: no remote copies, remote signals or barrier semaphores. Data moves between devices by JAX's collectives and lax.ppermute only.
A program may use at most 64 MiB of HBM per device.

v0:
```python
import math
import jax
import jax.numpy as jnp
from jax import lax
from jax.sharding import PartitionSpec as P

D_W = 8192
ITERS = 5
retain = 0.95
first_coef = 3.4445
second_coef = -4.775
third_coef = 2.0315
epsilon = 1e-07
shrink = 0.2


def swapped(block, axis, distance):
    count = lax.axis_size(axis)
    route = []
    for low in range(count):
        high = low | 1 << distance
        if high != low and high < count:
            route += [(low, high), (high, low)]
    return lax.ppermute(block, axis, route)


def on_device(features, key_partials, momentum):
    precise = lax.Precision.HIGHEST
    contract = (((0,), (0,)), ((), ()))
    parity = lax.axis_index("tp") % 2
    own_part = key_partials[:, 0, :]
    head_size = key_partials.shape[2]
    rows_half = momentum.shape[0]
    shard = lax.psum_scatter(
        lax.dot_general(features, own_part, contract, preferred_element_type=jnp.float32),
        "fsdp",
        scatter_dimension=0,
        tiled=True,
    )
    pieces = shard.reshape(2, rows_half, head_size)
    mine = jnp.where(parity == 0, pieces[0], pieces[1])
    other = jnp.where(parity == 0, pieces[1], pieces[0])
    grads = mine + swapped(other, "tp", 0)
    moment = momentum[:, 0, :]
    fresh = retain * moment + grads
    blend = grads + retain * fresh
    gram = lax.dot_general(blend, blend, contract, precision=precise)
    gram = lax.psum(gram, "fsdp")
    gram = gram + swapped(gram, "tp", 0)
    inverse = 1.0 / (jnp.sqrt(jnp.trace(gram)) + epsilon)
    state = blend * inverse
    gram = gram * (inverse * inverse)
    identity = jnp.eye(head_size, dtype=jnp.float32)
    for step in range(ITERS):
        square = jnp.dot(gram, gram, precision=precise)
        poly = first_coef * identity + second_coef * gram + third_coef * square
        state = jnp.dot(state, poly, precision=precise)
        gram = jnp.dot(poly, jnp.dot(gram, poly, precision=precise), precision=precise)
    update = shrink * math.sqrt(D_W) * state
    return (update[:, None, :], fresh[:, None, :])


def solution(mesh):
    placed = (P("fsdp", None), P("fsdp", "tp", None), P("fsdp", "tp", None))
    return jax.shard_map(
        on_device,
        mesh=mesh,
        in_specs=placed,
        out_specs=(P("fsdp", "tp", None), P("fsdp", "tp", None)),
        check_vma=False,
    )
```

profile of v0, /device:TPU:0, one launch (start us, length us, event | category | flops | bytes accessed | tf_op | source)
XLA Modules:
  0.0 150.5 jit_solution(14905172062143592151)
XLA Ops:
  7.2 0.0 copy-start
  7.2 0.0 reduce-scatter.2.cloned.1.call-start
  7.2 1.5 %copy-done = bf16[128,8192]{1,0:T(8,128)(2,1)S(1)} copy-done((bf16[128,8192]{1,0:T(8,128)(2,1)S(1)}, bf16[128,8192]{1,0:T(8,128)(2,1)}, u32[]{:S(2)}) %copy-start) | copy-done | bytes 2097176
  8.8 3.4 %fusion.14 = f32[8192,128]{1,0:T(8,128)} fusion(bf16[128,8192]{1,0:T(8,128)(2,1)S(1)} %copy-done, bf16[128,1,128]{2,0,1:T(8,128)(2,1)} %param.4), kind=kOutput, calls=%fused_computation.29 | convolution fusion | flops 268435456 | bytes 6324224 | tf_op jit(solution)/shard_map/dot_general | solution.py:35
  12.2 0.0 copy-start.1
  12.2 0.0 reduce-scatter.2.cloned.1.call-update
  12.2 0.0 all-reduce.2.cloned.1.call-start
  12.3 54.0 %reduce-scatter.2.cloned.1.call-done = f32[1024,128]{1,0:T(8,128)} async-done(((f32[8192,128]{1,0:T(8,128)}), f32[1024,128]{1,0:T(8,128)}) %reduce-scatter.2.cloned.1.call-update) | async-done | bytes 524304 | tf_op jit(solution)/shard_map/reduce_scatter | solution.py:34
  66.3 1.1 slice_select_fusion
  67.3 1.5 %collective-permute-start = (f32[512,128]{1,0:T(8,128)S(1)}, f32[512,128]{1,0:T(8,128)S(1)}, u32[]{:S(2)}, u32[]{:S(2)}) collective-permute-start(f32[512,128]{1,0:T(8,128)S(1)} %slice_select_fusion), channel_id=1, source_target_pairs={{0,1},{1,0},{2,3},{3,2},{4,5},{5,4},{6,7},{7,6},{8,9},{9,8},{10,11... | collective-permute-start | bytes 786440 | tf_op jit(solution)/shard_map/ppermute | solution.py:24
  68.9 6.4 %collective-permute-done = f32[512,128]{1,0:T(8,128)S(1)} collective-permute-done((f32[512,128]{1,0:T(8,128)S(1)}, f32[512,128]{1,0:T(8,128)S(1)}, u32[]{:S(2)}, u32[]{:S(2)}) %collective-permute-start) | collective-permute-done | bytes 262176 | tf_op jit(solution)/shard_map/ppermute | solution.py:24
  75.3 0.0 copy-done.1
  75.3 1.8 %bitcast_add_fusion = (f32[512,128]{1,0:T(8,128)}, f32[512,128]{1,0:T(8,128)S(1)}) fusion(f32[512,1,128]{2,0,1:T(8,128)S(1)} %bitcast.51, f32[512,128]{1,0:T(8,128)S(1)} %collective-permute-done, f32[1024,128]{1,0:T(8,128)} %reduce-scatter.2.cloned.1.call-done, pred[]{:T(512)S(6)} %eq.21), kind=kLoop, calls=%fused_computation.10 | loop fusion | flops 262144 | bytes 1572865 | tf_op jit(solution)/shard_map/add | solution.py:45
  77.1 1.2 fusion.7
  78.3 0.0 all-reduce.2.cloned.1.call-update
  78.3 53.3 %all-reduce.2.cloned.1.call-done = f32[128,128]{1,0:T(8,128)} async-done(((f32[128,128]{1,0:T(8,128)}), f32[128,128]{1,0:T(8,128)}) %all-reduce.2.cloned.1.call-update) | async-done | bytes 65552 | tf_op jit(solution)/shard_map/psum | solution.py:48
  131.7 1.5 collective-permute-start.1
  133.2 3.0 %collective-permute-done.1 = f32[128,128]{1,0:T(8,128)S(1)} collective-permute-done((f32[128,128]{1,0:T(8,128)}, f32[128,128]{1,0:T(8,128)S(1)}, u32[]{:S(2)}, u32[]{:S(2)}) %collective-permute-start.1) | collective-permute-done | bytes 65568 | tf_op jit(solution)/shard_map/ppermute | solution.py:24
  136.2 1.5 select_reduce_fusion
  138.4 0.2 fusion.8
  138.6 0.4 fusion.4
  139.0 0.2 fusion.9
  139.2 0.2 fusion.20
  139.4 0.2 fusion.3
  139.6 0.2 fusion.22
  139.8 0.4 fusion.21
  140.2 0.2 fusion.23
  140.4 0.2 fusion.2
  140.6 0.2 fusion.25
  140.8 0.4 fusion.24
  141.2 0.2 fusion.26
  141.4 0.2 fusion.1
  141.6 0.2 fusion.28
  141.8 0.4 fusion.27
  142.2 0.2 fusion.29
  142.4 0.2 fusion
  142.6 1.1 convolution_multiply_fusion
Async XLA Ops:
  7.2 1.6 %copy-start = (bf16[128,8192]{1,0:T(8,128)(2,1)S(1)}, bf16[128,8192]{1,0:T(8,128)(2,1)}, u32[]{:S(2)}) copy-start(bf16[128,8192]{1,0:T(8,128)(2,1)} %param.3) | copy-start | bytes 6291460
  7.2 59.1 %reduce-scatter.2.cloned.1.call-start = ((), (), s32[]{:S(2)}) async-start(), calls=%async_computation.1 | async-start | bytes 4718592 | tf_op jit(solution)/shard_map/reduce_scatter | solution.py:34
  12.2 63.1 %copy-start.1 = (f32[512,1,128]{2,1,0:T(1,128)S(1)}, f32[512,1,128]{2,1,0:T(1,128)}, u32[]{:S(2)}) copy-start(f32[512,1,128]{2,1,0:T(1,128)} %param.5) | copy-start | bytes 786436
  12.2 119.5 %all-reduce.2.cloned.1.call-start = ((), (), s32[]{:S(2)}) async-start(), calls=%async_computation.2 | async-start | bytes 131072 | tf_op jit(solution)/shard_map/psum | solution.py:48
  67.3 7.9 %collective-permute-start = (f32[512,128]{1,0:T(8,128)S(1)}, f32[512,128]{1,0:T(8,128)S(1)}, u32[]{:S(2)}, u32[]{:S(2)}) collective-permute-start(f32[512,128]{1,0:T(8,128)S(1)} %slice_select_fusion), channel_id=1, source_target_pairs={{0,1},{1,0},{2,3},{3,2},{4,5},{5,4},{6,7},{7,6},{8,9},{9,8},{10,11... | collective-permute-start | bytes 786440 | tf_op jit(solution)/shard_map/ppermute | solution.py:24
  131.7 4.5 %collective-permute-start.1 = (f32[128,128]{1,0:T(8,128)}, f32[128,128]{1,0:T(8,128)S(1)}, u32[]{:S(2)}, u32[]{:S(2)}) collective-permute-start(f32[128,128]{1,0:T(8,128)} %all-reduce.2.cloned.1.call-done), channel_id=1, source_target_pairs={{0,1},{1,0},{2,3},{3,2},{4,5},{5,4},{6,7},{7,6},{8,9},{9,8},{10,11... | collective-permute-start | bytes 196616 | tf_op jit(solution)/shard_map/ppermute | solution.py:24
Sparse Core Ops, SparseCore 0:
  12.4 53.8 reduce-scatter.1
  78.5 53.1 all-reduce.1
where the time goes:
time: 151 us
  waiting for transfers between devices  117 us (77%)
  between operations  14.9 us (10%)
  matrix products  9.86 us (7%)
  other arithmetic  4.35 us (3%)
  starting transfers between devices  3.11 us (2%)
  local copies, waits for them, and re-layouts  1.55 us (1%)
    reduce_scatter x1, waiting for transfers between devices, on_device(): lax.psum_scatter(lax.dot_general(features, own_part, contract, preferred_...  54 us
    psum x1, waiting for transfers between devices, on_device(): gram = lax.psum(gram, 'fsdp')  53.3 us
    ppermute x2, waiting for transfers between devices, swapped(): return lax.ppermute(block, axis, route)  9.37 us
    dot_general x1, matrix products, on_device(): lax.dot_general(features, own_part, contract, preferred_element_type=jnp....  3.45 us
    ppermute x2, starting transfers between devices, swapped(): return lax.ppermute(block, axis, route)  3.03 us
  transfers between devices with their start and end apart: 4, of which 4 were waited for; matrix products, arithmetic and copies ran while one was open for 0% of the time, Pallas kernels for 0%

commit v1 on v0

--- a/solution.py
+++ b/solution.py
@@ -45,7 +45,7 @@
     fresh = retain * moment + grads
     blend = grads + retain * fresh
     gram = lax.dot_general(blend, blend, contract, precision=precise)
-    gram = lax.psum(gram, "fsdp")
+    gram = jnp.sum(lax.all_gather(gram, "fsdp"), axis=0)
     gram = gram + swapped(gram, "tp", 0)
     inverse = 1.0 / (jnp.sqrt(jnp.trace(gram)) + epsilon)
     state = blend * inverse

time: 151 us -> 106 us (0.70)
  waiting for transfers between devices: 117 us -> 63.3 us
  blocking collectives: 0 us -> 9.81 us
    psum x1 -> x0, waiting for transfers between devices: 53.3 us -> none  [on_device(): gram = lax.psum(gram, 'fsdp')]
    all_gather x0 -> x1, blocking collectives: none -> 9.81 us  [on_device(): gram = jnp.sum(lax.all_gather(gram, 'fsdp'), axis=0)]
  transfers between devices with their start and end apart: 4 -> 3, of which waited for: 4 -> 3; matrix products, arithmetic and copies ran while one was open for 0% -> 0% of each run, Pallas kernels for 0% -> 0%
where the time goes in v1:
time: 106 us; the launch traced here: 105 us
  waiting for transfers between devices  63.3 us (60%)
  between operations  14.9 us (14%)
  blocking collectives  9.81 us (9%)
  matrix products  9.22 us (9%)
  other arithmetic  3.52 us (3%)
  starting transfers between devices  3.14 us (3%)
  local copies, waits for them, and re-layouts  1.55 us (1%)
    reduce_scatter x1, waiting for transfers between devices, on_device(): lax.psum_scatter(lax.dot_general(features, own_part, contract, preferred_...  54 us
    all_gather x1, blocking collectives, on_device(): gram = jnp.sum(lax.all_gather(gram, 'fsdp'), axis=0)  9.81 us
    ppermute x2, waiting for transfers between devices, swapped(): return lax.ppermute(block, axis, route)  9.24 us
    dot_general x1, matrix products, on_device(): lax.dot_general(features, own_part, contract, preferred_element_type=jnp....  3.45 us
    ppermute x2, starting transfers between devices, swapped(): return lax.ppermute(block, axis, route)  3.1 us
    dot_general x5, matrix products, on_device(): state = jnp.dot(state, poly, precision=precise)  2.52 us
  transfers between devices with their start and end apart: 3, of which 3 were waited for; matrix products, arithmetic and copies ran while one was open for 0% of the time, Pallas kernels for 0%

profile of v1, /device:TPU:0, one launch (start us, length us, event | category | flops | bytes accessed | tf_op | source)
XLA Modules:
  0.0 105.5 jit_solution(10197081606354440241)
XLA Ops:
  7.2 0.0 copy-start
  7.2 0.0 reduce-scatter.2.cloned.1.call-start
  7.2 1.5 %copy-done = bf16[128,8192]{1,0:T(8,128)(2,1)S(1)} copy-done((bf16[128,8192]{1,0:T(8,128)(2,1)S(1)}, bf16[128,8192]{1,0:T(8,128)(2,1)}, u32[]{:S(2)}) %copy-start) | copy-done | bytes 2097176
  8.8 3.4 %fusion.14 = f32[8192,128]{1,0:T(8,128)} fusion(bf16[128,8192]{1,0:T(8,128)(2,1)S(1)} %copy-done, bf16[128,1,128]{2,0,1:T(8,128)(2,1)} %param.4), kind=kOutput, calls=%fused_computation.29 | convolution fusion | flops 268435456 | bytes 6324224 | tf_op jit(solution)/shard_map/dot_general | solution.py:35
  12.2 0.0 copy-start.1
  12.2 0.0 reduce-scatter.2.cloned.1.call-update
  12.2 54.0 %reduce-scatter.2.cloned.1.call-done = f32[1024,128]{1,0:T(8,128)} async-done(((f32[8192,128]{1,0:T(8,128)}), f32[1024,128]{1,0:T(8,128)}) %reduce-scatter.2.cloned.1.call-update) | async-done | bytes 524304 | tf_op jit(solution)/shard_map/reduce_scatter | solution.py:34
  66.3 1.1 %slice_select_fusion = f32[512,128]{1,0:T(8,128)S(1)} fusion(f32[1024,128]{1,0:T(8,128)} %reduce-scatter.2.cloned.1.call-done, pred[]{:T(512)S(6)} %eq.21), kind=kLoop, calls=%fused_computation.15 | loop fusion | flops 65536 | bytes 786433 | tf_op jit(solution)/shard_map/jit(_where)/select_n | solution.py:42
  67.3 1.5 %collective-permute-start = (f32[512,128]{1,0:T(8,128)S(1)}, f32[512,128]{1,0:T(8,128)S(1)}, u32[]{:S(2)}, u32[]{:S(2)}) collective-permute-start(f32[512,128]{1,0:T(8,128)S(1)} %slice_select_fusion), channel_id=1, source_target_pairs={{0,1},{1,0},{2,3},{3,2},{4,5},{5,4},{6,7},{7,6},{8,9},{9,8},{10,11... | collective-permute-start | bytes 786440 | tf_op jit(solution)/shard_map/ppermute | solution.py:24
  68.9 6.4 %collective-permute-done = f32[512,128]{1,0:T(8,128)S(1)} collective-permute-done((f32[512,128]{1,0:T(8,128)S(1)}, f32[512,128]{1,0:T(8,128)S(1)}, u32[]{:S(2)}, u32[]{:S(2)}) %collective-permute-start) | collective-permute-done | bytes 262176 | tf_op jit(solution)/shard_map/ppermute | solution.py:24
  75.3 0.0 copy-done.1
  75.3 1.8 %bitcast_add_fusion = (f32[512,128]{1,0:T(8,128)}, f32[512,128]{1,0:T(8,128)S(1)}) fusion(f32[512,1,128]{2,0,1:T(8,128)S(1)} %bitcast.52, f32[512,128]{1,0:T(8,128)S(1)} %collective-permute-done, f32[1024,128]{1,0:T(8,128)} %reduce-scatter.2.cloned.1.call-done, pred[]{:T(512)S(6)} %eq.21), kind=kLoop, calls=%fused_computation.10 | loop fusion | flops 262144 | bytes 1572865 | tf_op jit(solution)/shard_map/add | solution.py:45
  77.1 0.6 fusion.7
  77.7 9.8 %all-gather = f32[1024,128]{1,0:T(8,128)S(1)} all-gather(f32[128,128]{1,0:T(8,128)S(1)} %fusion.7), channel_id=2, replica_groups=mesh['fsdp'=8,'tp'=4] {'fsdp'}, dimensions={0}, use_global_device_ids=true | all-gather | bytes 589824 | tf_op jit(solution)/shard_map/all_gather | solution.py:48
  87.5 1.6 %collective-permute-start.1 = (f32[128,128]{1,0:T(8,128)S(1)}, f32[128,128]{1,0:T(8,128)S(1)}, u32[]{:S(2)}, u32[]{:S(2)}) collective-permute-start(f32[128,128]{1,0:T(8,128)S(1)} %reduce_sum.19), channel_id=1, source_target_pairs={{0,1},{1,0},{2,3},{3,2},{4,5},{5,4},{6,7},{7,6},{8,9},{9,8},{10,11... | collective-permute-start | bytes 196616 | tf_op jit(solution)/shard_map/ppermute | solution.py:24
  89.1 2.9 %collective-permute-done.1 = f32[128,128]{1,0:T(8,128)S(1)} collective-permute-done((f32[128,128]{1,0:T(8,128)S(1)}, f32[128,128]{1,0:T(8,128)S(1)}, u32[]{:S(2)}, u32[]{:S(2)}) %collective-permute-start.1) | collective-permute-done | bytes 65568 | tf_op jit(solution)/shard_map/ppermute | solution.py:24
  92.0 0.6 select_reduce_fusion
  93.3 0.2 fusion.8
  93.5 0.4 fusion.4
  93.9 0.2 fusion.9
  94.1 0.2 fusion.20
  94.3 0.2 fusion.3
  94.5 0.2 fusion.22
  94.7 0.4 fusion.21
  95.1 0.2 fusion.23
  95.3 0.2 fusion.2
  95.5 0.2 fusion.25
  95.7 0.4 fusion.24
  96.1 0.2 fusion.26
  96.3 0.2 fusion.1
  96.5 0.2 fusion.28
  96.7 0.4 fusion.27
  97.1 0.2 fusion.29
  97.3 0.2 fusion
  97.5 1.1 %convolution_multiply_fusion = f32[512,128]{1,0:T(8,128)} fusion(f32[512,128]{1,0:T(8,128)S(1)} %fusion.27, f32[128,128]{1,0:T(8,128)S(1)} %fusion), kind=kOutput, calls=%fused_computation | convolution fusion | flops 100728832 | bytes 589824 | tf_op jit(solution)/shard_map/dot_general | solution.py:57
  (1 shorter events, 0.0 us)
Async XLA Ops:
  7.2 1.6 %copy-start = (bf16[128,8192]{1,0:T(8,128)(2,1)S(1)}, bf16[128,8192]{1,0:T(8,128)(2,1)}, u32[]{:S(2)}) copy-start(bf16[128,8192]{1,0:T(8,128)(2,1)} %param.3) | copy-start | bytes 6291460
  7.2 59.1 %reduce-scatter.2.cloned.1.call-start = ((), (), s32[]{:S(2)}) async-start(), calls=%async_computation.1 | async-start | bytes 4718592 | tf_op jit(solution)/shard_map/reduce_scatter | solution.py:34
  12.2 63.1 %copy-start.1 = (f32[512,1,128]{2,1,0:T(1,128)S(1)}, f32[512,1,128]{2,1,0:T(1,128)}, u32[]{:S(2)}) copy-start(f32[512,1,128]{2,1,0:T(1,128)} %param.5) | copy-start | bytes 786436
  67.3 7.9 %collective-permute-start = (f32[512,128]{1,0:T(8,128)S(1)}, f32[512,128]{1,0:T(8,128)S(1)}, u32[]{:S(2)}, u32[]{:S(2)}) collective-permute-start(f32[512,128]{1,0:T(8,128)S(1)} %slice_select_fusion), channel_id=1, source_target_pairs={{0,1},{1,0},{2,3},{3,2},{4,5},{5,4},{6,7},{7,6},{8,9},{9,8},{10,11... | collective-permute-start | bytes 786440 | tf_op jit(solution)/shard_map/ppermute | solution.py:24
  87.5 4.4 %collective-permute-start.1 = (f32[128,128]{1,0:T(8,128)S(1)}, f32[128,128]{1,0:T(8,128)S(1)}, u32[]{:S(2)}, u32[]{:S(2)}) collective-permute-start(f32[128,128]{1,0:T(8,128)S(1)} %reduce_sum.19), channel_id=1, source_target_pairs={{0,1},{1,0},{2,3},{3,2},{4,5},{5,4},{6,7},{7,6},{8,9},{9,8},{10,11... | collective-permute-start | bytes 196616 | tf_op jit(solution)/shard_map/ppermute | solution.py:24
Sparse Core Ops, SparseCore 0:
  12.4 53.8 reduce-scatter.1
